TPU v7x, 256 devices: a whole 4x4x8 slice. The times are simulated.
256 devices in a mesh: space: 128 (over x, y, z), chan: 2 (over core).
Axes of the slice: x: 4, y: 4, z: 8, core: 2. Of those that a mesh axis runs over, the one named last changes fastest.
Arguments:
- features: bfloat16 [262144, 256], P('space', 'chan'), may hold values from -6 to 6
- weights: bfloat16 [27, 256, 256], replicated, may hold values from -0.078125 to 0.078125
- cotangent: bfloat16 [262144, 256], P('space', 'chan'), may hold values from -6 to 6
- pair_offset: int32 [24576], P('space'), may hold values from 0 to 26
- pair_block: int32 [24576], P('space'), may hold values from 0 to 15
- pair_rows: int32 [24576, 128], P('space'), may hold values from 0 to 127
- pair_mask: int32 [24576, 128], P('space'), may hold values 0 or 1
- pair_dest_block: int32 [24576], P('space'), may hold values from 0 to 15
- remote_dest: int32 [16384, 1], P('space'), may hold values from 0 to 127; in each aligned block of 128 rows (0 to 127, 128 to 255, ...) at most 2 rows name the same one
Outputs:
- output: bfloat16 [262144, 256], P('space', 'chan')
- input_grad: bfloat16 [262144, 256], P('space', 'chan')
- weight_grad: float32 [27, 256, 256], P(None, None, 'chan')
Inputs may be any that keep to these rules, and one draw needn't show every extreme that they name: `remote_dest`: among the 128 remote entries of one index of space, no owner is named more than 2 times, and in some indices one owner is named exactly 2 times.
All inputs are finite; a program needn't handle non-finite values. No bound on the sum of `pair_mask` on one device may be relied on, other than what follows from the above.
Results may differ from a plain program's by a relative error of at most 0.009.
Values may be sent and summed in bfloat16 or wider, within the bound.
No kernel may reach another device: no remote copies, remote signals or barrier semaphores. Data moves between devices by JAX's collectives and lax.ppermute only.
A program may use at most 192 MiB of HBM per device.

v0:
```python
import jax
import jax.numpy as jnp
from jax import lax
from jax.sharding import PartitionSpec as P


def forward_local(
    rows, pair_kernels, pair_dest_block, local_count, block_count, block_rows, out_width
):
    product = jnp.einsum(
        "pri,pio->pro",
        rows[:local_count],
        pair_kernels[:local_count],
        preferred_element_type=jnp.float32,
    )
    resident = jnp.zeros((block_count, block_rows, out_width), jnp.float32)
    return resident.at[pair_dest_block[:local_count]].add(product)


def backward_terms(
    rows, upstream, pair_kernels, pair_offset, pair_mask, source, row_count, kernels
):
    in_width = pair_kernels.shape[1]
    out_width = pair_kernels.shape[2]
    back_term = jnp.einsum(
        "pro,pio->pri", upstream, pair_kernels, preferred_element_type=jnp.float32
    )
    back_term = back_term * pair_mask.astype(jnp.float32)[:, :, None]
    input_sum = (
        jnp.zeros((row_count, in_width), jnp.float32)
        .at[source.reshape(-1)]
        .add(back_term.reshape(-1, in_width))
    )
    outer_term = jnp.einsum("pri,pro->pio", rows, upstream, preferred_element_type=jnp.float32)
    weight_sum = (
        jnp.zeros((kernels, in_width, out_width), jnp.float32).at[pair_offset].add(outer_term)
    )
    return (input_sum, weight_sum)


def body(
    features,
    weights,
    cotangent,
    pair_offset,
    pair_block,
    pair_rows,
    pair_mask,
    pair_dest_block,
    remote_dest,
):
    space_count = lax.axis_size("space")
    chan_index = lax.axis_index("chan")
    row_count, half_width = features.shape
    kernels = weights.shape[0]
    pair_count, block_rows = pair_rows.shape
    remote_count = remote_dest.shape[0]
    local_count = pair_count - remote_count
    block_count = row_count // block_rows
    slot_depth = max(2, 2 * remote_count // space_count)
    block_ids = jnp.arange(block_count, dtype=jnp.int32)
    source = pair_block[:, None] * block_rows + pair_rows
    alive_rows = pair_mask.astype(jnp.bfloat16)[:, :, None]
    column_kernels = lax.dynamic_slice_in_dim(weights, chan_index * half_width, half_width, 2)
    pair_kernels = column_kernels[pair_offset]
    whole_rows = lax.all_gather(features, "chan", axis=1, tiled=True)
    gathered = whole_rows[source] * alive_rows
    moved_part = jnp.einsum(
        "pri,pio->pro",
        gathered[local_count:],
        pair_kernels[local_count:],
        preferred_element_type=jnp.float32,
    )
    resident = forward_local(
        gathered, pair_kernels, pair_dest_block, local_count, block_count, block_rows, half_width
    )
    sent_blocks = moved_part.astype(jnp.bfloat16)
    dest_device = remote_dest[:, 0]
    device_hits = (
        dest_device[:, None] == jnp.arange(space_count, dtype=jnp.int32)[None, :]
    ).astype(jnp.int32)
    rank_within = jnp.sum(jnp.cumsum(device_hits, axis=0) * device_hits, axis=1) - 1
    slot_index = dest_device * slot_depth + rank_within
    send_blocks = (
        jnp.zeros((space_count * slot_depth, block_rows, half_width), jnp.bfloat16)
        .at[slot_index]
        .set(sent_blocks)
    )
    send_targets = (
        jnp.full((space_count * slot_depth,), -1, jnp.int32)
        .at[slot_index]
        .set(pair_dest_block[local_count:])
    )
    recv_blocks, recv_targets = (
        lax.all_to_all(send_blocks, "space", split_axis=0, concat_axis=0, tiled=True),
        lax.all_to_all(send_targets, "space", split_axis=0, concat_axis=0, tiled=True),
    )
    arrival = (recv_targets[None, :] == block_ids[:, None]).astype(jnp.bfloat16)
    remote_sum = jnp.einsum("bs,sro->bro", arrival, recv_blocks, preferred_element_type=jnp.float32)
    output = (resident + remote_sum).reshape(row_count, half_width).astype(jnp.bfloat16)
    safe_targets = jnp.clip(recv_targets, 0, block_count - 1)
    live_slots = (recv_targets >= 0)[:, None, None]
    cot_blocks = cotangent.reshape(block_count, block_rows, half_width)
    wanted = cot_blocks[safe_targets]
    back_send = jnp.where(live_slots, wanted, jnp.zeros_like(wanted))
    back_recv = lax.all_to_all(back_send, "space", split_axis=0, concat_axis=0, tiled=True)
    upstream = jnp.concatenate(
        [cot_blocks[pair_dest_block[:local_count]], back_recv[slot_index]], axis=0
    )
    input_sum, weight_sum = backward_terms(
        gathered, upstream, pair_kernels, pair_offset, pair_mask, source, row_count, kernels
    )
    input_grad = lax.psum_scatter(
        input_sum.astype(jnp.bfloat16), "chan", scatter_dimension=1, tiled=True
    )
    grad_scale = (kernels / (pair_count * space_count * block_rows)) ** 0.5
    weight_grad = lax.psum(weight_sum, "space") * grad_scale
    return (output, input_grad, weight_grad)


def solution(mesh):
    in_specs = (
        P("space", "chan"),
        P(),
        P("space", "chan"),
        P("space"),
        P("space"),
        P("space", None),
        P("space", None),
        P("space"),
        P("space", None),
    )
    out_specs = (P("space", "chan"), P("space", "chan"), P(None, None, "chan"))
    return jax.shard_map(body, mesh=mesh, in_specs=in_specs, out_specs=out_specs, check_vma=False)
```

profile of v0, /device:TPU:2, one launch (start us, length us, event | category | flops | bytes accessed | tf_op | source)
XLA Modules:
  0.0 747.1 jit_solution(18217090853142078470)
XLA Ops:
  7.2 0.7 all-gather.2.cloned.1.call-update
  7.9 1.7 fusion.22
  9.6 1.6 reduce_window_sum.11
  11.2 1.0 select_reduce_fusion
  12.2 0.7 fusion.26
  12.9 0.8 slice.19
  13.7 1.0 scatter_custom_fusion
  14.6 0.8 all_to_all.12
  15.4 16.0 %all-to-all-start = ((s32[128,2,1]{1,2,0:T(1,128)}), s32[128,2,1]{1,2,0:T(1,128)}, u32[]{:S(2)}, u32[]{:S(2)}) async-start(s32[128,2,1]{1,2,0:T(1,128)} %bitcast.39), calls=%async_computation | async-start | bytes 131072 | tf_op jit(solution)/shard_map/all_to_all | solution.py:96
  31.4 0.7 compare_select_fusion.4
  32.1 0.7 broadcast_multiply_fusion.2
  32.8 1.6 fusion.29
  34.4 0.7 compare_select_fusion.3
  35.1 0.5 copy-done.7
  35.6 1.5 constant_dynamic-slice_fusion
  37.2 9.7 %gather_fusion.1 = bf16[192,256,128]{2,1,0:T(8,128)(2,1)} fusion(bf16[27,256,128]{2,1,0:T(8,128)(2,1)} %constant_dynamic-slice_fusion, s32[1024]{0:T(1024)S(1)} %pad_clamp_fusion.3), kind=kCustom, calls=%fused_computation.1 | custom fusion | bytes 25166592 | tf_op jit(solution)/shard_map/gather | solution.py:65
  46.9 7.8 %fusion.39 = bf16[128,256,128]{2,1,0:T(8,128)(2,1)} fusion(bf16[192,256,128]{2,1,0:T(8,128)(2,1)} %gather_fusion.1), kind=kLoop, calls=%fused_computation.17.clone.clone.clone.2 | loop fusion | bytes 16777216 | tf_op jit(solution)/shard_map/pri,pio->pro/dot_general | solution.py:68
  54.8 0.7 compare_select_fusion
  55.5 0.6 pad_clamp_fusion
  56.1 0.6 broadcast.150
  56.7 1.8 clamp_reduce_fusion
  58.9 1.0 gather_fusion.2
  59.8 8.4 %gather_fusion.3 = bf16[256,128,128]{2,1,0:T(8,128)(2,1)} fusion(bf16[16,128,128]{2,1,0:T(8,128)(2,1)S(1)} %bitcast.30, s32[1024]{0:T(1024)S(1)} %get-tuple-element.9), kind=kCustom, calls=%fused_computation.3 | custom fusion | bytes 16778240 | tf_op jit(solution)/shard_map/gather | solution.py:104
  68.2 7.3 broadcast_select_fusion
  75.5 14.3 %all-to-all-start.2 = ((bf16[256,128,128]{2,1,0:T(8,128)(2,1)}), bf16[256,128,128]{2,1,0:T(8,128)(2,1)}, u32[]{:S(2)}, u32[]{:S(2)}) async-start(bf16[256,128,128]{2,1,0:T(8,128)(2,1)} %broadcast_select_fusion), calls=%async_computation.2 | async-start | bytes 16777216 | tf_op jit(solution)/shard_map/all_to_all | solution.py:106
  89.8 1.6 constant_dynamic-update-slice_fusion.1
  91.3 92.1 %gather_fusion = bf16[24576,256]{1,0:T(8,128)(2,1)} fusion(bf16[2048,256]{1,0:T(8,128)(2,1)} %all-gather.2.cloned.1.call-done, s32[24576]{0:T(1024)S(1)} %get-tuple-element.5), kind=kCustom, calls=%fused_computation | custom fusion | bytes 25264128 | tf_op jit(solution)/shard_map/gather | solution.py:67
  183.4 9.3 %fusion.13 = bf16[128,128,128]{2,1,0:T(8,128)(2,1)} fusion(bf16[192,128,256]{2,1,0:T(8,128)(2,1)} %bitcast.31, bf16[192,128]{1,0:T(8,128)(2,1)S(1)} %copy-done.5, bf16[128,256,128]{2,1,0:T(8,128)(2,1)} %fusion.39), kind=kOutput, calls=%fused_computation.25 | convolution fusion | flops 1101004800 | bytes 25214976 | tf_op jit(solution)/shard_map/pri,pio->pro/dot_general | solution.py:68
  192.7 5.3 broadcast.104
  198.0 19.4 %scatter_fusion = bf16[256,128,128]{2,1,0:T(8,128)(2,1)} fusion(bf16[256,128,128]{2,1,0:T(8,128)(2,1)} %broadcast.104, s32[128]{0:T(128)S(1)} %copy-done.14, bf16[128,128,128]{2,1,0:T(8,128)(2,1)} %fusion.13), kind=kCustom, calls=%fused_computation.6 | custom fusion | bytes 12583424 | tf_op jit(solution)/shard_map/scatter | solution.py:87
  217.4 58.1 %all-to-all-done.2 = bf16[256,128,128]{2,1,0:T(8,128)(2,1)} async-done(((bf16[256,128,128]{2,1,0:T(8,128)(2,1)}), bf16[256,128,128]{2,1,0:T(8,128)(2,1)}, u32[]{:S(2)}, u32[]{:S(2)}) %all-to-all-start.2) | async-done | bytes 8388640 | tf_op jit(solution)/shard_map/all_to_all | solution.py:106
  275.5 9.9 %all-to-all-start.1 = ((bf16[256,128,128]{2,1,0:T(8,128)(2,1)}), bf16[256,128,128]{2,1,0:T(8,128)(2,1)}, u32[]{:S(2)}, u32[]{:S(2)}) async-start(bf16[256,128,128]{2,1,0:T(8,128)(2,1)} %scatter_fusion), calls=%async_computation.1 | async-start | bytes 16777216 | tf_op jit(solution)/shard_map/all_to_all | solution.py:95
  285.5 6.5 gather_fusion.4
  292.1 4.8 constant_dynamic-update-slice_fusion
  296.9 13.8 %broadcast_multiply_fusion = f32[192,128,256]{2,1,0:T(8,128)} fusion(f32[192,128]{1,0:T(8,128)S(1)} %copy-done.4, bf16[192,128,128]{2,1,0:T(8,128)(2,1)} %constant_dynamic-update-slice_fusion, bf16[192,256,128]{2,1,0:T(8,128)(2,1)} %gather_fusion.1), kind=kOutput, calls=%fused_computation.10 | convolution fusion | flops 1616904192 | bytes 44138496 | tf_op jit(solution)/shard_map/pro,pio->pri/dot_general | solution.py:25
  310.7 132.4 %scatter_custom_fusion.3 = f32[2048,256]{1,0:T(8,128)S(1)} fusion(s32[24576]{0:T(1024)} %bitcast.40, f32[24576,256]{1,0:T(8,128)} %bitcast.34, f32[]{:T(128)} %constant.23.clone.1), kind=kCustom, calls=%fused_computation.27 | custom fusion | flops 6291456 | bytes 2097664 | tf_op jit(solution)/shard_map/scatter-add | solution.py:32
  443.1 1.4 copy.24
  444.7 18.3 %fusion = f32[192,256,128]{2,1,0:T(8,128)} fusion(bf16[192,128,128]{2,1,0:T(8,128)(2,1)} %constant_dynamic-update-slice_fusion, bf16[192,128,256]{2,1,0:T(8,128)(2,1)} %bitcast.32, bf16[192,128]{1,0:T(8,128)(2,1)S(1)} %copy-done.5), kind=kOutput, calls=%fused_computation.11 | convolution fusion | flops 1616904192 | bytes 44089344 | tf_op jit(solution)/shard_map/pri,pro->pio/dot_general | solution.py:34
  463.4 36.3 %scatter_fusion.2 = f32[27,256,128]{2,1,0:T(8,128)S(1)} fusion(f32[27,256,128]{2,1,0:T(8,128)S(1)} %broadcast_in_dim.26, s32[192]{0:T(256)S(1)} %copy-done.8, f32[192,256,128]{2,1,0:T(8,128)} %fusion), kind=kCustom, calls=%fused_computation.9 | custom fusion | flops 6291456 | bytes 75498240 | tf_op jit(solution)/shard_map/scatter-add | solution.py:36
  499.7 1.8 copy-done.2
  501.5 6.0 fusion.2
  507.5 7.9 %fusion.7 = f32[16,128,128]{2,0,1:T(8,128)S(1)} fusion(bf16[256,128,128]{2,1,0:T(8,128)(2,1)} %all-to-all-done.1, s32[256]{0:T(256)S(1)} %copy-done.10), kind=kOutput, calls=%fused_computation.18 | convolution fusion | flops 134221824 | bytes 9438208 | tf_op jit(solution)/shard_map/bs,sro->bro/dot_general | solution.py:99
  515.3 1.4 copy.21
  516.7 13.5 %scatter_fusion.1 = f32[16,128,128]{2,1,0:T(8,128)} fusion(f32[16,128,128]{2,1,0:T(8,128)} %copy.21, s32[64]{0:T(128)S(1)} %copy-done.12, f32[64,128,128]{2,1,0:T(8,128)} %fusion.2), kind=kCustom, calls=%fused_computation.7 | custom fusion | flops 1048576 | bytes 12583168 | tf_op jit(solution)/shard_map/scatter-add | solution.py:17
  530.3 2.1 convert_element_type.25
  532.4 2.0 copy.25
  534.4 201.9 %all-reduce.2.cloned.1.call-done = f32[27,256,128]{2,1,0:T(8,128)} async-done(((f32[27,256,128]{2,1,0:T(8,128)}), f32[27,256,128]{2,1,0:T(8,128)}) %all-reduce.2.cloned.1.call-update) | async-done | bytes 3538960 | tf_op jit(solution)/shard_map/psum | solution.py:117
  736.4 4.2 broadcast_multiply_fusion.1
  (46 shorter events, 1.1 us)
Async XLA Ops:
  7.2 28.4 %copy-start = (bf16[27,256,256]{2,1,0:T(8,128)(2,1)S(1)}, bf16[27,256,256]{2,1,0:T(8,128)(2,1)}, u32[]{:S(2)}) copy-start(bf16[27,256,256]{2,1,0:T(8,128)(2,1)} %param.10) | copy-start | bytes 10616836
  7.2 84.1 %all-gather.2.cloned.1.call-start = ((), (), s32[]{:S(2)}) async-start(), calls=%async_computation.4 | async-start | bytes 1572864 | tf_op jit(solution)/shard_map/all_gather | solution.py:66
  12.9 42.6 %copy-start.13 = (s32[128]{0:T(128)}, s32[128]{0:T(128)S(1)}, u32[]{:S(2)}) copy-start(s32[128]{0:T(128)S(1)} %fusion.26) | copy-start | bytes 1540
  15.4 40.7 %all-to-all-start = ((s32[128,2,1]{1,2,0:T(1,128)}), s32[128,2,1]{1,2,0:T(1,128)}, u32[]{:S(2)}, u32[]{:S(2)}) async-start(s32[128,2,1]{1,2,0:T(1,128)} %bitcast.39), calls=%async_computation | async-start | bytes 131072 | tf_op jit(solution)/shard_map/all_to_all | solution.py:96
  32.1 26.8 %copy-start.11 = (s32[64]{0:T(128)}, s32[64]{0:T(128)S(1)}, u32[]{:S(2)}) copy-start(s32[64]{0:T(128)S(1)} %compare_select_fusion.4) | copy-start | bytes 772
  35.1 0.5 copy-start.7
  46.9 7.8 %copy-start.6 = (s32[192,128]{1,0:T(8,128)S(1)}, s32[192,128]{1,0:T(8,128)}, u32[]{:S(2)}) copy-start(s32[192,128]{1,0:T(8,128)} %param.14) | copy-start | bytes 294916
  46.9 12.0 %copy-start.3 = (bf16[2048,128]{1,0:T(8,128)(2,1)S(1)}, bf16[2048,128]{1,0:T(8,128)(2,1)}, u32[]{:S(2)}) copy-start(bf16[2048,128]{1,0:T(8,128)(2,1)} %param.11) | copy-start | bytes 1572868
  58.7 9.6 %copy-start.9 = (s32[256]{0:T(256)}, s32[256]{0:T(256)S(1)}, u32[]{:S(2)}) copy-start(s32[256]{0:T(256)S(1)} %eq.34) | copy-start | bytes 3076
  75.5 200.0 %all-to-all-start.2 = ((bf16[256,128,128]{2,1,0:T(8,128)(2,1)}), bf16[256,128,128]{2,1,0:T(8,128)(2,1)}, u32[]{:S(2)}, u32[]{:S(2)}) async-start(bf16[256,128,128]{2,1,0:T(8,128)(2,1)} %broadcast_select_fusion), calls=%async_computation.2 | async-start | bytes 16777216 | tf_op jit(solution)/shard_map/all_to_all | solution.py:106
  91.3 92.1 %copy-start.5 = (bf16[192,128]{1,0:T(8,128)(2,1)S(1)}, bf16[192,128]{1,0:T(8,128)(2,1)}, u32[]{:S(2)}) copy-start(bf16[192,128]{1,0:T(8,128)(2,1)} %get-tuple-element.8) | copy-start | bytes 147460
  192.7 5.3 copy-start.14
  275.5 231.9 %all-to-all-start.1 = ((bf16[256,128,128]{2,1,0:T(8,128)(2,1)}), bf16[256,128,128]{2,1,0:T(8,128)(2,1)}, u32[]{:S(2)}, u32[]{:S(2)}) async-start(bf16[256,128,128]{2,1,0:T(8,128)(2,1)} %scatter_fusion), calls=%async_computation.1 | async-start | bytes 16777216 | tf_op jit(solution)/shard_map/all_to_all | solution.py:95
  285.5 11.4 %copy-start.4 = (f32[192,128]{1,0:T(8,128)S(1)}, f32[192,128]{1,0:T(8,128)}, u32[]{:S(2)}) copy-start(f32[192,128]{1,0:T(8,128)} %get-tuple-element.7) | copy-start | bytes 294916
  285.5 246.9 %reduce-scatter.4.cloned.1.call-start = ((), (), s32[]{:S(2)}) async-start(), calls=%async_computation.6 | async-start | bytes 1572864
  444.6 18.7 %copy-start.8 = (s32[192]{0:T(256)S(1)}, s32[192]{0:T(256)}, u32[]{:S(2)}) copy-start(s32[192]{0:T(256)} %copy-done.7) | copy-start | bytes 2308
  444.6 291.8 %all-reduce.2.cloned.1.call-start = ((), (), s32[]{:S(2)}) async-start(), calls=%async_computation.5 | async-start | bytes 7077888 | tf_op jit(solution)/shard_map/psum | solution.py:117
  499.7 1.8 copy-start.2
  501.5 6.0 copy-start.10
  507.5 9.3 %copy-start.12 = (s32[64]{0:T(128)S(1)}, s32[64]{0:T(128)}, u32[]{:S(2)}) copy-start(s32[64]{0:T(128)} %copy-done.11) | copy-start | bytes 772
  515.3 225.2 %copy-start.1 = (bf16[27,256,256]{2,1,0:T(8,128)(2,1)S(1)}, bf16[27,256,256]{2,1,0:T(8,128)(2,1)}, u32[]{:S(2)}) copy-start(bf16[27,256,256]{2,1,0:T(8,128)(2,1)} %param.10) | copy-start | bytes 10616836
Sparse Core Ops, SparseCore 0:
  9.8 17.0 all-gather.1
  444.7 14.9 reduce-scatter.3
  501.6 234.7 all-reduce.1
where the time goes:
time: 749 us; the launch traced here: 747 us
  waiting for transfers between devices  261 us (35%)
  other arithmetic  208 us (28%)
  local copies, waits for them, and re-layouts  169 us (23%)
  matrix products  55.2 us (7%)
  starting transfers between devices  40.3 us (5%)
  between operations  14 us (2%)
    psum x1, waiting for transfers between devices, body(): weight_grad = lax.psum(weight_sum, 'space') * grad_scale  202 us
    scatter-add x1, other arithmetic, backward_terms(): input_sum = jnp.zeros((row_count, in_width), jnp.float32).at[source.resha...  132 us
    gather x1, local copies, waits for them, and re-layouts, body(): gathered = whole_rows[source] * alive_rows  92.1 us
    all_to_all x1, waiting for transfers between devices, body(): lax.all_to_all(back_send, 'space', split_axis=0, concat_axis=0, tiled=True)  58.1 us
    scatter-add x1, other arithmetic, backward_terms(): jnp.zeros((kernels, in_width, out_width), jnp.float32).at[pair_offset]  36.3 us
    scatter x1, local copies, waits for them, and re-layouts, body(): send_blocks = jnp.zeros((space_count * slot_depth, block_rows, half_width...  19.4 us
    dot_general x1, matrix products, backward_terms(): jnp.einsum('pri,pro->pio', rows, upstream, preferred_element_type=jnp.flo...  18.3 us
    all_to_all x1, starting transfers between devices, body(): lax.all_to_all(send_targets, 'space', split_axis=0, concat_axis=0, tiled=...  16 us
  transfers between devices with their start and end apart: 6, of which 2 were waited for; matrix products, arithmetic and copies ran while one was open for 57% of the time, Pallas kernels for 0%

commit v1 on v0

v1 whole, which is shorter than its diff:
```python
import jax
import jax.numpy as jnp
from jax import lax
from jax.experimental import pallas as pl
from jax.experimental.pallas import tpu as pltpu
from jax.sharding import Mesh
from jax.sharding import PartitionSpec as P

SPACE = ("x", "y", "z")
PLANE = ("x", "y")
FACTORS = {128: (4, 4, 8), 8: (2, 2, 2)}
BF16 = jnp.bfloat16
F32 = jnp.float32

VM = pl.BlockSpec(memory_space=pltpu.VMEM)
SM = pl.BlockSpec(memory_space=pltpu.SMEM)


def pick_transposed(rows_ref, at, block_rows):
    rows = rows_ref[pl.ds(at, 1), :]
    lines = lax.broadcasted_iota(jnp.int32, (block_rows, rows.shape[1]), 0)
    return jnp.where(lines == rows, 1.0, 0.0).astype(BF16)


def forward_block(picked, feats, kernel):
    rows = lax.dot_general(
        picked, feats, (((0,), (0,)), ((), ())), preferred_element_type=F32
    ).astype(BF16)
    return jnp.dot(rows, kernel, preferred_element_type=F32)


def backward_block(picked, upstream, feats_t, kernel, in_ref, block, w_ref, offset):
    spread = jnp.dot(picked, upstream, preferred_element_type=F32).astype(BF16)
    in_ref[block] += lax.dot_general(
        spread, kernel, (((1,), (1,)), ((), ())), preferred_element_type=F32
    )
    w_ref[offset] += jnp.dot(feats_t, spread, preferred_element_type=F32)


def send_kernel(offset, block, slot, rows_ref, feat_ref, kern_ref, first_ref, last_ref):
    half = first_ref.shape[1]

    def step(q, carry):
        picked = pick_transposed(rows_ref, q, feat_ref.shape[1])
        part = forward_block(picked, feat_ref[block[q]], kern_ref[offset[q]]).astype(BF16)
        first_ref[slot[q]] = part[:half]
        last_ref[slot[q]] = part[half:]
        return carry

    lax.fori_loop(0, rows_ref.shape[0], step, 0, unroll=4)


def pack_kernel(code, cot_ref, out_ref):
    def step(s, carry):
        out_ref[s] = cot_ref[code[s]]
        return carry

    lax.fori_loop(0, out_ref.shape[0], step, 0, unroll=8)


def local_kernel(
    offset, block, dest, rows_ref, feat_ref, feat_t_ref, kern_ref, cot_ref, res_ref, in_ref, w_ref
):
    res_ref[...] = jnp.zeros_like(res_ref)
    in_ref[...] = jnp.zeros_like(in_ref)
    w_ref[...] = jnp.zeros_like(w_ref)

    def step(q, carry):
        b, k, d = block[q], offset[q], dest[q]
        picked = pick_transposed(rows_ref, q, feat_ref.shape[1])
        kernel = kern_ref[k]
        res_ref[d] += forward_block(picked, feat_ref[b], kernel)
        backward_block(picked, cot_ref[d], feat_t_ref[b], kernel, in_ref, b, w_ref, k)
        return carry

    lax.fori_loop(0, rows_ref.shape[0], step, 0, unroll=2)


def remote_kernel(
    offset, block, slot, rows_ref, feat_t_ref, kern_ref, up_ref, in0_ref, w0_ref, in_ref, w_ref
):
    in_ref[...] = in0_ref[...]
    w_ref[...] = w0_ref[...]

    def step(q, carry):
        b, k = block[q], offset[q]
        picked = pick_transposed(rows_ref, q, feat_t_ref.shape[2])
        backward_block(
            picked, up_ref[slot[q]], feat_t_ref[b], kern_ref[k], in_ref, b, w_ref, k
        )
        return carry

    lax.fori_loop(0, rows_ref.shape[0], step, 0, unroll=4)


def column_kernel(code, recv_ref, out_ref, acc_ref):
    acc_ref[...] = jnp.zeros_like(acc_ref)

    def step(s, carry):
        acc_ref[code[s]] += recv_ref[s].astype(F32)
        return carry

    lax.fori_loop(0, recv_ref.shape[0], step, 0, unroll=4)

    def put(b, carry):
        out_ref[b] = acc_ref[b].astype(BF16)
        return carry

    lax.fori_loop(0, out_ref.shape[0], put, 0, unroll=8)


def call(kernel, scalars, arrays, outs, scratch=(), flops=0):
    moved = sum(a.size * a.dtype.itemsize for a in arrays)
    moved += sum(o.size * o.dtype.itemsize for o in outs)
    return pl.pallas_call(
        kernel,
        out_shape=outs,
        in_specs=[SM] * len(scalars) + [VM] * len(arrays),
        out_specs=[VM] * len(outs),
        scratch_shapes=list(scratch),
        cost_estimate=pl.CostEstimate(flops=flops, bytes_accessed=moved, transcendentals=0),
    )(*scalars, *arrays)


def after(a, *others):
    return lax.optimization_barrier((a,) + others)[0]


def plane_exchange(a):
    return lax.all_to_all(a, PLANE, split_axis=0, concat_axis=0, tiled=True)


def reduce_weights(total, kernels, in_width, out_width, ahead, last):
    columns = lax.axis_size("z")
    planes = lax.axis_size("x") * lax.axis_size("y")
    flat = total.reshape(kernels * in_width, out_width).astype(BF16)
    part = after(lax.psum_scatter(flat, "z", scatter_dimension=0, tiled=True), ahead)
    rows = part.shape[0]
    each = -(-rows // (planes * 16)) * 16
    part = jnp.pad(part, ((0, planes * each - rows), (0, 0)))
    pieces = plane_exchange(part).reshape(planes, each, out_width)
    summed = jnp.sum(pieces.astype(F32), axis=0).astype(BF16)
    spread = jnp.broadcast_to(summed[None], (planes, each, out_width))
    whole = plane_exchange(spread.reshape(planes * each, out_width))[:rows]
    return lax.all_gather(after(whole, last), "z", axis=0, tiled=True).astype(F32)


def body(
    features,
    weights,
    cotangent,
    pair_offset,
    pair_block,
    pair_rows,
    pair_mask,
    pair_dest_block,
    remote_dest,
):
    columns = lax.axis_size("z")
    planes = lax.axis_size("x") * lax.axis_size("y")
    chan = lax.axis_index("chan")
    row_count, width = features.shape
    kernels, in_width, _ = weights.shape
    pair_count, rows = pair_rows.shape
    remote = remote_dest.shape[0]
    local = pair_count - remote
    blocks = row_count // rows
    depth = 2 * columns
    slots = planes * depth
    half = rows // 2

    dest = remote_dest[:, 0]
    plane_of = dest // columns
    wanted = (dest % columns) * blocks + pair_dest_block[local:]
    order = jnp.arange(remote, dtype=jnp.int32)
    same = (plane_of[:, None] == plane_of[None, :]) & (order[None, :] < order[:, None])
    slot = plane_of * depth + jnp.sum(same.astype(jnp.int32), axis=1)
    hits = slot[None, :] == jnp.arange(slots, dtype=jnp.int32)[:, None]
    sent_code = jnp.max(jnp.where(hits, wanted[None, :], -1), axis=1)
    code = plane_exchange(sent_code)

    picks = jnp.where(pair_mask > 0, pair_rows, rows)
    kern = lax.dynamic_slice_in_dim(weights, chan * width, width, 2)
    other = lax.ppermute(features, "chan", [(0, 1), (1, 0)])
    low = jnp.where(chan == 0, features, other)
    high = jnp.where(chan == 0, other, features)
    feats = jnp.concatenate([low, high], axis=1).reshape(blocks, rows, in_width)

    sent = call(
        send_kernel,
        (pair_offset[local:], pair_block[local:], slot),
        (picks[local:], feats, kern),
        [
            jax.ShapeDtypeStruct((slots, half, width), BF16),
            jax.ShapeDtypeStruct((slots, rows - half, width), BF16),
        ],
        flops=2 * remote * rows * in_width * (rows + width),
    )
    came_first = plane_exchange(after(sent[0], code))
    column_cot = lax.all_gather(cotangent, "z", axis=0, tiled=True)

    feats_t = jnp.swapaxes(feats, 1, 2)
    resident, in_sum, w_sum = call(
        local_kernel,
        (pair_offset[:local], pair_block[:local], pair_dest_block[:local]),
        (after(picks[:local], sent[0]), feats, feats_t, kern, cotangent.reshape(blocks, rows, width)),
        [
            jax.ShapeDtypeStruct((blocks, rows, width), F32),
            jax.ShapeDtypeStruct((blocks, rows, in_width), F32),
            jax.ShapeDtypeStruct((kernels, in_width, width), F32),
        ],
        flops=2 * local * rows * in_width * (rows + width) * 2,
    )

    valid_code = jnp.maximum(code, 0)
    sum_code = jnp.where(code < 0, columns * blocks, code)
    packed = call(
        pack_kernel,
        (after(valid_code, resident),),
        (column_cot.reshape(columns * blocks, rows, width),),
        [jax.ShapeDtypeStruct((slots, rows, width), BF16)],
    )[0]
    upstream = plane_exchange(after(packed, came_first))

    def column_total(came):
        return call(
            column_kernel,
            (sum_code,),
            (came,),
            [jax.ShapeDtypeStruct((columns * blocks,) + came.shape[1:], BF16)],
            [pltpu.VMEM((columns * blocks + 1,) + came.shape[1:], F32)],
        )[0]

    first_total = column_total(came_first)
    first_sum = lax.psum_scatter(first_total, "z", scatter_dimension=0, tiled=True)
    came_last = plane_exchange(after(sent[1], upstream, first_total))

    in_sum, w_sum = call(
        remote_kernel,
        (pair_offset[local:], pair_block[local:], slot),
        (picks[local:], feats_t, kern, after(upstream, first_sum), in_sum, w_sum),
        [
            jax.ShapeDtypeStruct((blocks, rows, in_width), F32),
            jax.ShapeDtypeStruct((kernels, in_width, width), F32),
        ],
        flops=2 * remote * rows * in_width * (rows + width),
    )
    last_total = column_total(came_last)
    last_sum = lax.psum_scatter(last_total, "z", scatter_dimension=0, tiled=True)

    grad_scale = (kernels / (pair_count * columns * planes * rows)) ** 0.5
    weight_grad = reduce_weights(w_sum, kernels, in_width, width, last_total, last_sum) * grad_scale
    weight_grad = weight_grad.reshape(kernels, in_width, width)

    in_sum = in_sum.reshape(row_count, in_width)
    mine = lax.dynamic_slice_in_dim(in_sum, chan * width, width, 1)
    theirs = lax.dynamic_slice_in_dim(in_sum, (1 - chan) * width, width, 1)
    theirs = lax.ppermute(theirs.astype(BF16), "chan", [(0, 1), (1, 0)])
    input_grad = (mine + theirs.astype(F32)).astype(BF16)

    output = resident + jnp.concatenate([first_sum, last_sum], axis=1).astype(F32)
    output = output.reshape(row_count, width).astype(BF16)
    return (output, input_grad, weight_grad)


def solution(mesh):
    x, y, z = FACTORS[mesh.devices.shape[0]]
    split = Mesh(mesh.devices.reshape(x, y, z, -1), SPACE + ("chan",))
    in_specs = (
        P(SPACE, "chan"),
        P(),
        P(SPACE, "chan"),
        P(SPACE),
        P(SPACE),
        P(SPACE, None),
        P(SPACE, None),
        P(SPACE),
        P(SPACE, None),
    )
    out_specs = (P(SPACE, "chan"), P(SPACE, "chan"), P(None, None, "chan"))
    return jax.shard_map(body, mesh=split, in_specs=in_specs, out_specs=out_specs, check_vma=False)
```

time: 749 us -> 445 us (0.59)
  other arithmetic: 208 us -> 18.8 us
  local copies, waits for them, and re-layouts: 169 us -> 13.5 us
  Pallas kernels: 0 us -> 93.8 us
  matrix products: 55.2 us -> 0 us
  waiting for transfers between devices: 261 us -> 211 us
  starting transfers between devices: 40.3 us -> 67.1 us
  blocking collectives: 0 us -> 25.8 us
    psum x1 -> x0, waiting for transfers between devices: 202 us -> none  [body(): weight_grad = lax.psum(weight_sum, 'space') * grad_scale]
    scatter-add x3 -> x0, other arithmetic: 182 us -> none  [the longest x1 132 us: backward_terms(): input_sum = jnp.zeros((row_count, in_width), jnp.float32).at[source.resha...]
    gather x5 -> x0, local copies, waits for them, and re-layouts: 118 us -> none  [the longest x1 92.1 us: body(): gathered = whole_rows[source] * alive_rows]
    pallas_call x0 -> x6, Pallas kernels: none -> 93.8 us  [call(): pl.pallas_call(kernel, out_shape=outs, in_specs=[SM] * len(scalars) + [VM...]
    all_to_all x3 -> x4, waiting for transfers between devices: 58.1 us -> 130 us  [plane_exchange(): return lax.all_to_all(a, PLANE, split_axis=0, concat_axis=0, tiled=True)]
    dot_general x5 -> x0, matrix products: 55.2 us -> none  [the longest x1 18.3 us: backward_terms(): jnp.einsum('pri,pro->pio', rows, upstream, preferred_element_type=jnp.flo...]
    reduce_scatter x0 -> x3, waiting for transfers between devices: none -> 45.5 us  [the longest x1 28.7 us: reduce_weights(): lax.psum_scatter(flat, 'z', scatter_dimension=0, tiled=True)]
    all_gather x1 -> x2, waiting for transfers between devices: 0.01 us -> 32.3 us  [the longest x1 32.3 us: reduce_weights(): lax.all_gather(after(whole, last), 'z', axis=0, tiled=True).astype(F32)]
  transfers between devices with their start and end apart: 6 -> 11, of which waited for: 2 -> 7; matrix products, arithmetic and copies ran while one was open for 57% -> 6% of each run, Pallas kernels for 0% -> 21%
where the time goes in v1:
time: 445 us; the launch traced here: 444 us
  waiting for transfers between devices  211 us (47%)
  Pallas kernels  93.8 us (21%)
  starting transfers between devices  67.1 us (15%)
  blocking collectives  25.8 us (6%)
  other arithmetic  18.8 us (4%)
  between operations  13.9 us (3%)
  local copies, waits for them, and re-layouts  13.5 us (3%)
    all_to_all x4, waiting for transfers between devices, plane_exchange(): return lax.all_to_all(a, PLANE, split_axis=0, concat_axis=0, tiled=True)  130 us
    pallas_call x6, Pallas kernels, call(): pl.pallas_call(kernel, out_shape=outs, in_specs=[SM] * len(scalars) + [VM...  93.8 us
    all_to_all x4, starting transfers between devices, plane_exchange(): return lax.all_to_all(a, PLANE, split_axis=0, concat_axis=0, tiled=True)  66.7 us
    all_gather x1, waiting for transfers between devices, reduce_weights(): lax.all_gather(after(whole, last), 'z', axis=0, tiled=True).astype(F32)  32.3 us
    reduce_scatter x1, waiting for transfers between devices, reduce_weights(): lax.psum_scatter(flat, 'z', scatter_dimension=0, tiled=True)  28.7 us
    all_to_all x2, blocking collectives, plane_exchange(): return lax.all_to_all(a, PLANE, split_axis=0, concat_axis=0, tiled=True)  25.8 us
    reduce_scatter x1, waiting for transfers between devices, body(): lax.psum_scatter(last_total, 'z', scatter_dimension=0, tiled=True)  16.8 us
  transfers between devices with their start and end apart: 11, of which 7 were waited for; matrix products, arithmetic and copies ran while one was open for 6% of the time, Pallas kernels for 21%

profile of v1, /device:TPU:2, one launch (start us, length us, event | category | flops | bytes accessed | tf_op | source)
XLA Modules:
  0.0 443.7 jit_solution(2487843596938370189)
XLA Ops:
  7.2 0.7 all-gather.3.cloned.1.call-update
  7.9 0.1 collective-permute-start
  8.0 0.9 fusion.3
  8.9 0.8 fusion.2
  9.7 0.2 convert_reduce_fusion
  9.9 0.1 select_reduce_fusion
  10.0 0.7 all_to_all.29
  10.7 7.5 %all-to-all-start = ((s32[16,16,1]{1,2,0:T(1,128)}), s32[16,16,1]{1,2,0:T(1,128)S(1)}, u32[]{:S(2)}, u32[]{:S(2)}) async-start(s32[16,16,1]{1,2,0:T(1,128)} %bitcast.5), calls=%async_computation | async-start | bytes 16384 | tf_op jit(solution)/shard_map/all_to_all | solution.py:130
  18.1 1.6 compare_select_fusion
  19.7 1.6 constant_dynamic-slice_fusion.kern_ref
  21.3 0.6 slice.34.offset
  21.9 1.3 slice.35.block
  23.2 1.5 slice.40.rows_ref
  24.7 0.5 broadcast.110
  25.2 0.7 reduce.5
  26.0 1.3 broadcast_select_fusion.1
  27.3 1.1 pad_maximum_fusion
  28.4 18.9 %shard_map.112 = (bf16[256,64,128]{2,1,0:T(8,128)(2,1)}, bf16[256,64,128]{2,1,0:T(8,128)(2,1)}) custom-call(s32[128]{0:T(128)} %slice.34.offset, s32[128]{0:T(128)} %slice.35.block, s32[128]{0:T(128)} %copy-done.3, s32[128,128]{1,0:T(8,128)} %slice.40.rows_ref, bf16[16,128,256]{2,1,0:T(8,128)(2,1)} %bitcast.33, ...), custom_call_target="tpu_custom_call" | custom-call | flops 2147483648 | bytes 11272192 | tf_op jit(solution)/shard_map/pallas_call | solution.py:115
  47.2 7.4 %all-to-all-start.1 = ((bf16[256,64,128]{2,1,0:T(8,128)(2,1)}), bf16[256,64,128]{2,1,0:T(8,128)(2,1)}, u32[]{:S(2)}, u32[]{:S(2)}) async-start(bf16[256,64,128]{2,1,0:T(8,128)(2,1)} %get-tuple-element.21), calls=%async_computation.1 | async-start | bytes 8388608 | tf_op jit(solution)/shard_map/all_to_all | solution.py:130
  54.6 0.5 slice.30.offset
  55.1 0.5 slice.31.block
  55.6 0.5 slice.32.dest
  56.2 1.4 slice.39.rows_ref
  57.5 0.6 broadcast_maximum_fusion
  58.1 1.3 copy.17
  59.4 23.6 %shard_map.113 = (f32[16,128,128]{2,1,0:T(8,128)}, f32[16,128,256]{2,1,0:T(8,128)}, f32[27,256,128]{2,1,0:T(8,128)}) custom-call(s32[64]{0:T(128)} %slice.30.offset, s32[64]{0:T(128)} %slice.31.block, s32[64]{0:T(128)} %slice.32.dest, s32[64,128]{1,0:T(8,128)} %slice.39.rows_ref, bf16[16,128,256]{2,1,0:T(8,128)(2,1)} %bitcast.34, ...), custom_call_target="tpu_custom_call" | custom-call | flops 2147483648 | bytes 11108352 | tf_op jit(solution)/shard_map/pallas_call | solution.py:115
  83.0 6.1 %shard_map.115 = bf16[256,128,128]{2,1,0:T(8,128)(2,1)} custom-call(s32[256]{0:T(256)} %get-tuple-element.23.code, bf16[128,128,128]{2,1,0:T(8,128)(2,1)} %bitcast.30), custom_call_target="tpu_custom_call" | custom-call | bytes 12582912 | tf_op jit(solution)/shard_map/pallas_call | solution.py:115
  89.1 19.9 %all-to-all-done.1.recv_ref = bf16[256,64,128]{2,1,0:T(8,128)(2,1)} async-done(((bf16[256,64,128]{2,1,0:T(8,128)(2,1)}), bf16[256,64,128]{2,1,0:T(8,128)(2,1)}, u32[]{:S(2)}, u32[]{:S(2)}) %all-to-all-start.1) | async-done | bytes 4194336 | tf_op jit(solution)/shard_map/all_to_all | solution.py:130
  109.0 17.6 %all-to-all-start.2 = ((bf16[256,128,128]{2,1,0:T(8,128)(2,1)}), bf16[256,128,128]{2,1,0:T(8,128)(2,1)}, u32[]{:S(2)}, u32[]{:S(2)}) async-start(bf16[256,128,128]{2,1,0:T(8,128)(2,1)} %shard_map.115), calls=%async_computation.3 | async-start | bytes 16777216 | tf_op jit(solution)/shard_map/all_to_all | solution.py:130
  126.6 5.6 %shard_map.114 = bf16[128,64,128]{2,1,0:T(8,128)(2,1)} custom-call(s32[256]{0:T(256)} %get-tuple-element.36.code, bf16[256,64,128]{2,1,0:T(8,128)(2,1)} %all-to-all-done.1.recv_ref), custom_call_target="tpu_custom_call" | custom-call | bytes 6291456 | tf_op jit(solution)/shard_map/pallas_call | solution.py:115
  132.3 100.8 %all-to-all-done.2.up_ref = bf16[256,128,128]{2,1,0:T(8,128)(2,1)} async-done(((bf16[256,128,128]{2,1,0:T(8,128)(2,1)}), bf16[256,128,128]{2,1,0:T(8,128)(2,1)}, u32[]{:S(2)}, u32[]{:S(2)}) %all-to-all-start.2) | async-done | bytes 8388640 | tf_op jit(solution)/shard_map/all_to_all | solution.py:130
  233.0 34.3 %all-to-all-start.3 = ((bf16[256,64,128]{2,1,0:T(8,128)(2,1)}), bf16[256,64,128]{2,1,0:T(8,128)(2,1)}, u32[]{:S(2)}, u32[]{:S(2)}) async-start(bf16[256,64,128]{2,1,0:T(8,128)(2,1)} %get-tuple-element.25), calls=%async_computation.4 | async-start | bytes 8388608 | tf_op jit(solution)/shard_map/all_to_all | solution.py:130
  267.4 34.0 %shard_map.117 = (f32[16,128,256]{2,1,0:T(8,128)}, f32[27,256,128]{2,1,0:T(8,128)}) custom-call(s32[128]{0:T(128)} %slice.34.offset, s32[128]{0:T(128)} %slice.35.block, s32[128]{0:T(128)} %copy-done.3, s32[128,128]{1,0:T(8,128)} %slice.40.rows_ref, bf16[16,256,128]{2,1,0:T(8,128)(2,1)} %bitcast.32, ...), custom_call_target="tpu_custom_call" | custom-call | flops 2147483648 | bytes 22544384 | tf_op jit(solution)/shard_map/pallas_call | solution.py:115
  301.4 3.6 convert_element_type.41
  305.0 9.6 %all-to-all-done.3.recv_ref = bf16[256,64,128]{2,1,0:T(8,128)(2,1)} async-done(((bf16[256,64,128]{2,1,0:T(8,128)(2,1)}), bf16[256,64,128]{2,1,0:T(8,128)(2,1)}, u32[]{:S(2)}, u32[]{:S(2)}) %all-to-all-start.3) | async-done | bytes 4194336 | tf_op jit(solution)/shard_map/all_to_all | solution.py:130
  314.7 5.6 %shard_map.116 = bf16[128,64,128]{2,1,0:T(8,128)(2,1)} custom-call(s32[256]{0:T(256)} %get-tuple-element.36.code, bf16[256,64,128]{2,1,0:T(8,128)(2,1)} %all-to-all-done.3.recv_ref), custom_call_target="tpu_custom_call" | custom-call | bytes 6291456 | tf_op jit(solution)/shard_map/pallas_call | solution.py:115
  320.4 28.7 %reduce-scatter.8.cloned.1.call-done = bf16[864,128]{1,0:T(8,128)(2,1)} async-done(((bf16[6912,128]{1,0:T(8,128)(2,1)}), bf16[864,128]{1,0:T(8,128)(2,1)}) %reduce-scatter.8.cloned.1.call-update) | async-done | bytes 221200 | tf_op jit(solution)/shard_map/reduce_scatter | solution.py:137
  349.1 1.0 pad.4
  350.0 13.9 %all_to_all.45 = bf16[16,64,128]{2,1,0:T(8,128)(2,1)S(1)} all-to-all(bf16[16,64,128]{2,1,0:T(8,128)(2,1)S(1)} %bitcast.39), channel_id=1, replica_groups=mesh['x'=4,'y'=4,'z'=8,'chan'=2] {'x','y'}, dimensions={0} | all-to-all | bytes 524288 | tf_op jit(solution)/shard_map/all_to_all | solution.py:130
  364.0 11.9 %all_to_all.46 = bf16[16,64,128]{2,1,0:T(8,128)(2,1)S(1)} all-to-all(bf16[16,64,128]{2,1,0:T(8,128)(2,1)S(1)} %broadcast_in_dim.37), channel_id=1, replica_groups=mesh['x'=4,'y'=4,'z'=8,'chan'=2] {'x','y'}, dimensions={0} | all-to-all | bytes 524288 | tf_op jit(solution)/shard_map/all_to_all | solution.py:130
  375.9 0.7 slice.41
  376.7 16.8 %reduce-scatter.6.cloned.1.call-done = bf16[16,64,128]{2,1,0:T(8,128)(2,1)} async-done(((bf16[128,64,128]{2,1,0:T(8,128)(2,1)}), bf16[16,64,128]{2,1,0:T(8,128)(2,1)}) %reduce-scatter.6.cloned.1.call-update) | async-done | bytes 262160 | tf_op jit(solution)/shard_map/reduce_scatter | solution.py:249
  393.5 1.3 dynamic-slice_convert_fusion
  394.9 1.9 collective-permute-done.1
  396.8 2.3 add_convert_fusion
  399.1 2.3 add_convert_fusion.1
  401.3 32.3 %all-gather.5.cloned.1.call-done = bf16[6912,128]{1,0:T(8,128)(2,1)} async-done(((bf16[864,128]{1,0:T(8,128)(2,1)}), bf16[6912,128]{1,0:T(8,128)(2,1)}) %all-gather.5.cloned.1.call-update) | async-done | bytes 1769488 | tf_op jit(solution)/shard_map/all_gather | solution.py:145
  433.7 3.5 convert_multiply_fusion
  (32 shorter events, 0.6 us)
Async XLA Ops:
  7.2 12.6 %copy-start = (bf16[27,256,256]{2,1,0:T(8,128)(2,1)S(1)}, bf16[27,256,256]{2,1,0:T(8,128)(2,1)}, u32[]{:S(2)}) copy-start(bf16[27,256,256]{2,1,0:T(8,128)(2,1)} %param.10) | copy-start | bytes 10616836
  7.2 14.1 %copy-start.5 = (s32[192]{0:T(256)S(1)}, s32[192]{0:T(256)}, u32[]{:S(2)}) copy-start(s32[192]{0:T(256)} %param.12) | copy-start | bytes 2308
  7.2 75.8 %all-gather.3.cloned.1.call-start = ((), (), s32[]{:S(2)}) async-start(), calls=%async_computation.10 | async-start | bytes 4718592 | tf_op jit(solution)/shard_map/all_gather | solution.py:200
  7.9 18.1 %collective-permute-start = (bf16[2048,128]{1,0:T(8,128)(2,1)}, bf16[2048,128]{1,0:T(8,128)(2,1)}, u32[]{:S(2)}, u32[]{:S(2)}) collective-permute-start(bf16[2048,128]{1,0:T(8,128)(2,1)} %param.9), channel_id=1, source_target_pairs={{0,1},{1,0},{2,3},{3,2},{4,5},{5,4},{6,7},{7,6},{8,9},{9,8},{10,11... | collective-permute-start | bytes 1572872 | tf_op jit(solution)/shard_map/ppermute | solution.py:184
  9.9 18.5 %copy-start.3 = (s32[128]{0:T(128)}, s32[128]{0:T(128)S(1)}, u32[]{:S(2)}) copy-start(s32[128]{0:T(128)S(1)} %multiply_add_fusion.slot) | copy-start | bytes 1540
  10.7 14.0 %all-to-all-start = ((s32[16,16,1]{1,2,0:T(1,128)}), s32[16,16,1]{1,2,0:T(1,128)S(1)}, u32[]{:S(2)}, u32[]{:S(2)}) async-start(s32[16,16,1]{1,2,0:T(1,128)} %bitcast.5), calls=%async_computation | async-start | bytes 16384 | tf_op jit(solution)/shard_map/all_to_all | solution.py:130
  47.2 7.9 %copy-start.6 = (s32[192]{0:T(256)S(1)}, s32[192]{0:T(256)}, u32[]{:S(2)}) copy-start(s32[192]{0:T(256)} %param.13) | copy-start | bytes 2308
  47.2 8.4 %copy-start.4 = (s32[192]{0:T(256)S(1)}, s32[192]{0:T(256)}, u32[]{:S(2)}) copy-start(s32[192]{0:T(256)} %param.16) | copy-start | bytes 2308
  47.2 10.9 %copy-start.2 = (bf16[2048,256]{1,0:T(8,128)(2,1)S(1)}, bf16[2048,256]{1,0:T(8,128)(2,1)}, u32[]{:S(2)}) copy-start(bf16[2048,256]{1,0:T(8,128)(2,1)} %pad_maximum_fusion) | copy-start | bytes 3145732
  47.2 61.8 %all-to-all-start.1 = ((bf16[256,64,128]{2,1,0:T(8,128)(2,1)}), bf16[256,64,128]{2,1,0:T(8,128)(2,1)}, u32[]{:S(2)}, u32[]{:S(2)}) async-start(bf16[256,64,128]{2,1,0:T(8,128)(2,1)} %get-tuple-element.21), calls=%async_computation.1 | async-start | bytes 8388608 | tf_op jit(solution)/shard_map/all_to_all | solution.py:130
  109.0 124.1 %all-to-all-start.2 = ((bf16[256,128,128]{2,1,0:T(8,128)(2,1)}), bf16[256,128,128]{2,1,0:T(8,128)(2,1)}, u32[]{:S(2)}, u32[]{:S(2)}) async-start(bf16[256,128,128]{2,1,0:T(8,128)(2,1)} %shard_map.115), calls=%async_computation.3 | async-start | bytes 16777216 | tf_op jit(solution)/shard_map/all_to_all | solution.py:130
  126.6 140.8 %reduce-scatter.4.cloned.1.call-start = ((), (), s32[]{:S(2)}) async-start(), calls=%async_computation.9 | async-start | bytes 2359296 | tf_op jit(solution)/shard_map/reduce_scatter | solution.py:235
  233.0 81.6 %all-to-all-start.3 = ((bf16[256,64,128]{2,1,0:T(8,128)(2,1)}), bf16[256,64,128]{2,1,0:T(8,128)(2,1)}, u32[]{:S(2)}, u32[]{:S(2)}) async-start(bf16[256,64,128]{2,1,0:T(8,128)(2,1)} %get-tuple-element.25), calls=%async_computation.4 | async-start | bytes 8388608 | tf_op jit(solution)/shard_map/all_to_all | solution.py:130
  267.3 81.7 %reduce-scatter.8.cloned.1.call-start = ((), (), s32[]{:S(2)}) async-start(), calls=%async_computation.12 | async-start | bytes 1990656 | tf_op jit(solution)/shard_map/reduce_scatter | solution.py:137
  305.0 88.5 %reduce-scatter.6.cloned.1.call-start = ((), (), s32[]{:S(2)}) async-start(), calls=%async_computation.11 | async-start | bytes 2359296 | tf_op jit(solution)/shard_map/reduce_scatter | solution.py:249
  320.3 113.4 %all-gather.5.cloned.1.call-start = ((), (), s32[]{:S(2)}) async-start(), calls=%async_computation.13 | async-start | bytes 1990656 | tf_op jit(solution)/shard_map/all_gather | solution.py:145
  394.8 2.0 collective-permute-start.1
  396.8 40.4 %copy-start.1 = (bf16[27,256,256]{2,1,0:T(8,128)(2,1)S(1)}, bf16[27,256,256]{2,1,0:T(8,128)(2,1)}, u32[]{:S(2)}) copy-start(bf16[27,256,256]{2,1,0:T(8,128)(2,1)} %param.10) | copy-start | bytes 10616836
Sparse Core Ops, SparseCore 0:
  9.8 57.6 all-gather.2
  132.4 44.8 reduce-scatter.3
  305.1 43.9 reduce-scatter.7
  352.0 41.3 reduce-scatter.5
  395.1 38.5 all-gather.4

commit v2 on v1

--- a/solution.py
+++ b/solution.py
@@ -37,17 +37,21 @@
     w_ref[offset] += jnp.dot(feats_t, spread, preferred_element_type=F32)
 
 
-def send_kernel(offset, block, slot, rows_ref, feat_ref, kern_ref, first_ref, last_ref):
-    half = first_ref.shape[1]
-
+def send_kernel(offset, block, rows_ref, feat_ref, kern_ref, out_ref):
     def step(q, carry):
         picked = pick_transposed(rows_ref, q, feat_ref.shape[1])
-        part = forward_block(picked, feat_ref[block[q]], kern_ref[offset[q]]).astype(BF16)
-        first_ref[slot[q]] = part[:half]
-        last_ref[slot[q]] = part[half:]
+        out_ref[q] = forward_block(picked, feat_ref[block[q]], kern_ref[offset[q]]).astype(BF16)
         return carry
 
     lax.fori_loop(0, rows_ref.shape[0], step, 0, unroll=4)
+
+
+def place_kernel(slot, part_ref, out_ref):
+    def step(q, carry):
+        out_ref[slot[q]] = part_ref[q]
+        return carry
+
+    lax.fori_loop(0, part_ref.shape[0], step, 0, unroll=8)
 
 
 def pack_kernel(code, cot_ref, out_ref):
@@ -130,19 +134,12 @@
     return lax.all_to_all(a, PLANE, split_axis=0, concat_axis=0, tiled=True)
 
 
-def reduce_weights(total, kernels, in_width, out_width, ahead, last):
-    columns = lax.axis_size("z")
-    planes = lax.axis_size("x") * lax.axis_size("y")
-    flat = total.reshape(kernels * in_width, out_width).astype(BF16)
-    part = after(lax.psum_scatter(flat, "z", scatter_dimension=0, tiled=True), ahead)
-    rows = part.shape[0]
-    each = -(-rows // (planes * 16)) * 16
-    part = jnp.pad(part, ((0, planes * each - rows), (0, 0)))
-    pieces = plane_exchange(part).reshape(planes, each, out_width)
+def spread_weights(pieces, planes):
     summed = jnp.sum(pieces.astype(F32), axis=0).astype(BF16)
-    spread = jnp.broadcast_to(summed[None], (planes, each, out_width))
-    whole = plane_exchange(spread.reshape(planes * each, out_width))[:rows]
-    return lax.all_gather(after(whole, last), "z", axis=0, tiled=True).astype(F32)
+    columns = lax.all_gather(summed, "z", axis=0, tiled=False)
+    whole = jnp.sum(columns.astype(F32), axis=0).astype(BF16)
+    copies = jnp.broadcast_to(whole[None], (planes,) + whole.shape)
+    return plane_exchange(copies.reshape(-1, whole.shape[1]))
 
 
 def body(
@@ -166,18 +163,24 @@
     local = pair_count - remote
     blocks = row_count // rows
     depth = 2 * columns
-    slots = planes * depth
-    half = rows // 2
+    shallow = depth * 3 // 4
+
+    column_cot = lax.all_gather(cotangent, "z", axis=0, tiled=True)
+    column_cot = column_cot.reshape(columns * blocks, rows, width)
 
     dest = remote_dest[:, 0]
     plane_of = dest // columns
     wanted = (dest % columns) * blocks + pair_dest_block[local:]
     order = jnp.arange(remote, dtype=jnp.int32)
     same = (plane_of[:, None] == plane_of[None, :]) & (order[None, :] < order[:, None])
-    slot = plane_of * depth + jnp.sum(same.astype(jnp.int32), axis=1)
-    hits = slot[None, :] == jnp.arange(slots, dtype=jnp.int32)[:, None]
+    rank = jnp.sum(same.astype(jnp.int32), axis=1)
+    slot = plane_of * depth + rank
+    hits = slot[None, :] == jnp.arange(planes * depth, dtype=jnp.int32)[:, None]
     sent_code = jnp.max(jnp.where(hits, wanted[None, :], -1), axis=1)
     code = plane_exchange(sent_code)
+    most = jnp.broadcast_to(jnp.max(rank), (planes * columns,))
+    most = lax.all_to_all(after(most, code), SPACE, split_axis=0, concat_axis=0, tiled=True)
+    fits = jnp.max(most) < shallow
 
     picks = jnp.where(pair_mask > 0, pair_rows, rows)
     kern = lax.dynamic_slice_in_dim(weights, chan * width, width, 2)
@@ -185,81 +188,74 @@
     low = jnp.where(chan == 0, features, other)
     high = jnp.where(chan == 0, other, features)
     feats = jnp.concatenate([low, high], axis=1).reshape(blocks, rows, in_width)
-
-    sent = call(
+    feats_t = jnp.swapaxes(feats, 1, 2)
+    cot_blocks = cotangent.reshape(blocks, rows, width)
+    sums = [
+        jax.ShapeDtypeStruct((blocks, rows, in_width), F32),
+        jax.ShapeDtypeStruct((kernels, in_width, width), F32),
+    ]
+
+    parts = call(
         send_kernel,
-        (pair_offset[local:], pair_block[local:], slot),
+        (pair_offset[local:], pair_block[local:]),
         (picks[local:], feats, kern),
-        [
-            jax.ShapeDtypeStruct((slots, half, width), BF16),
-            jax.ShapeDtypeStruct((slots, rows - half, width), BF16),
-        ],
+        [jax.ShapeDtypeStruct((remote, rows, width), BF16)],
         flops=2 * remote * rows * in_width * (rows + width),
+    )[0]
+
+    def exchange(deep):
+        slots = planes * deep
+        place = plane_of * deep + rank
+        codes = code.reshape(planes, depth)[:, :deep].reshape(slots)
+        boxes = [jax.ShapeDtypeStruct((slots, rows, width), BF16)]
+
+        packed = call(pack_kernel, (jnp.maximum(codes, 0),), (column_cot,), boxes)[0]
+        upstream = plane_exchange(packed)
+
+        resident, in_sum, w_sum = call(
+            local_kernel,
+            (pair_offset[:local], pair_block[:local], pair_dest_block[:local]),
+            (after(picks[:local], packed), feats, feats_t, kern, cot_blocks),
+            [jax.ShapeDtypeStruct((blocks, rows, width), F32)] + sums,
+            flops=4 * local * rows * in_width * (rows + width),
+        )
+        placed = call(place_kernel, (place,), (after(parts, packed),), boxes)[0]
+        came = plane_exchange(after(placed, upstream, resident))
+
+        in_sum, w_sum = call(
+            remote_kernel,
+            (pair_offset[local:], pair_block[local:], place),
+            (picks[local:], feats_t, kern, upstream, in_sum, w_sum),
+            sums,
+            flops=2 * remote * rows * in_width * (rows + width),
+        )
+        flat = w_sum.reshape(kernels * in_width, width).astype(BF16)
+        pieces = plane_exchange(after(flat, came))
+        column_sum = call(
+            column_kernel,
+            (jnp.where(codes < 0, columns * blocks, codes),),
+            (came,),
+            [jax.ShapeDtypeStruct((columns * blocks, rows, width), BF16)],
+            [pltpu.VMEM((columns * blocks + 1, rows, width), F32)],
+        )[0]
+        return resident, in_sum, pieces, column_sum
+
+    resident, in_sum, pieces, column_sum = lax.cond(
+        fits, lambda: exchange(shallow), lambda: exchange(depth)
     )
-    came_first = plane_exchange(after(sent[0], code))
-    column_cot = lax.all_gather(cotangent, "z", axis=0, tiled=True)
-
-    feats_t = jnp.swapaxes(feats, 1, 2)
-    resident, in_sum, w_sum = call(
-        local_kernel,
-        (pair_offset[:local], pair_block[:local], pair_dest_block[:local]),
-        (after(picks[:local], sent[0]), feats, feats_t, kern, cotangent.reshape(blocks, rows, width)),
-        [
-            jax.ShapeDtypeStruct((blocks, rows, width), F32),
-            jax.ShapeDtypeStruct((blocks, rows, in_width), F32),
-            jax.ShapeDtypeStruct((kernels, in_width, width), F32),
-        ],
-        flops=2 * local * rows * in_width * (rows + width) * 2,
-    )
-
-    valid_code = jnp.maximum(code, 0)
-    sum_code = jnp.where(code < 0, columns * blocks, code)
-    packed = call(
-        pack_kernel,
-        (after(valid_code, resident),),
-        (column_cot.reshape(columns * blocks, rows, width),),
-        [jax.ShapeDtypeStruct((slots, rows, width), BF16)],
-    )[0]
-    upstream = plane_exchange(after(packed, came_first))
-
-    def column_total(came):
-        return call(
-            column_kernel,
-            (sum_code,),
-            (came,),
-            [jax.ShapeDtypeStruct((columns * blocks,) + came.shape[1:], BF16)],
-            [pltpu.VMEM((columns * blocks + 1,) + came.shape[1:], F32)],
-        )[0]
-
-    first_total = column_total(came_first)
-    first_sum = lax.psum_scatter(first_total, "z", scatter_dimension=0, tiled=True)
-    came_last = plane_exchange(after(sent[1], upstream, first_total))
-
-    in_sum, w_sum = call(
-        remote_kernel,
-        (pair_offset[local:], pair_block[local:], slot),
-        (picks[local:], feats_t, kern, after(upstream, first_sum), in_sum, w_sum),
-        [
-            jax.ShapeDtypeStruct((blocks, rows, in_width), F32),
-            jax.ShapeDtypeStruct((kernels, in_width, width), F32),
-        ],
-        flops=2 * remote * rows * in_width * (rows + width),
-    )
-    last_total = column_total(came_last)
-    last_sum = lax.psum_scatter(last_total, "z", scatter_dimension=0, tiled=True)
+
+    arrived = lax.psum_scatter(column_sum, "z", scatter_dimension=0, tiled=True)
+    output = (resident + arrived.astype(F32)).reshape(row_count, width).astype(BF16)
 
     grad_scale = (kernels / (pair_count * columns * planes * rows)) ** 0.5
-    weight_grad = reduce_weights(w_sum, kernels, in_width, width, last_total, last_sum) * grad_scale
-    weight_grad = weight_grad.reshape(kernels, in_width, width)
+    whole = spread_weights(pieces.reshape(planes, -1, width), planes)
+    weight_grad = (whole.astype(F32) * grad_scale).reshape(kernels, in_width, width)
 
     in_sum = in_sum.reshape(row_count, in_width)
     mine = lax.dynamic_slice_in_dim(in_sum, chan * width, width, 1)
     theirs = lax.dynamic_slice_in_dim(in_sum, (1 - chan) * width, width, 1)
     theirs = lax.ppermute(theirs.astype(BF16), "chan", [(0, 1), (1, 0)])
     input_grad = (mine + theirs.astype(F32)).astype(BF16)
-
-    output = resident + jnp.concatenate([first_sum, last_sum], axis=1).astype(F32)
-    output = output.reshape(row_count, width).astype(BF16)
     return (output, input_grad, weight_grad)
 
 

time: 445 us -> 386 us (0.87)
  waiting for transfers between devices: 211 us -> 119 us
  blocking collectives: 25.8 us -> 66.9 us
  starting transfers between devices: 67.1 us -> 56 us
    all_gather x0 -> x1, blocking collectives: none -> 66.9 us  [spread_weights(): columns = lax.all_gather(summed, 'z', axis=0, tiled=False)]
    reduce_scatter x3 -> x1, waiting for transfers between devices: 45.5 us -> 0.01 us  [body(): arrived = lax.psum_scatter(column_sum, 'z', scatter_dimension=0, tiled=True)]
    all_gather x1 -> x0, waiting for transfers between devices: 32.3 us -> none  [reduce_weights(): lax.all_gather(after(whole, last), 'z', axis=0, tiled=True).astype(F32)]
    all_to_all x2 -> x0, blocking collectives: 25.8 us -> none  [plane_exchange(): return lax.all_to_all(a, PLANE, split_axis=0, concat_axis=0, tiled=True)]
    all_to_all x4 -> x5, starting transfers between devices: 66.7 us -> 42.7 us  [plane_exchange(): return lax.all_to_all(a, PLANE, split_axis=0, concat_axis=0, tiled=True)]
    all_to_all x4 -> x5, waiting for transfers between devices: 130 us -> 110 us  [plane_exchange(): return lax.all_to_all(a, PLANE, split_axis=0, concat_axis=0, tiled=True)]
    all_to_all x0 -> x1, starting transfers between devices: none -> 13.1 us  [body(): lax.all_to_all(after(most, code), SPACE, split_axis=0, concat_axis=0, til...]
    all_to_all x0 -> x1, waiting for transfers between devices: none -> 6.43 us  [body(): lax.all_to_all(after(most, code), SPACE, split_axis=0, concat_axis=0, til...]
  transfers between devices with their start and end apart: 11 -> 10, of which waited for: 7 -> 7; matrix products, arithmetic and copies ran while one was open for 6% -> 9% of each run, Pallas kernels for 21% -> 22%
where the time goes in v2:
time: 386 us; the launch traced here: 385 us
  waiting for transfers between devices  119 us (31%)
  Pallas kernels  89.9 us (23%)
  blocking collectives  66.9 us (17%)
  starting transfers between devices  56 us (15%)
  other arithmetic  22.5 us (6%)
  local copies, waits for them, and re-layouts  15.1 us (4%)
  between operations  14.9 us (4%)
    all_to_all x5, waiting for transfers between devices, plane_exchange(): return lax.all_to_all(a, PLANE, split_axis=0, concat_axis=0, tiled=True)  110 us
    pallas_call x6, Pallas kernels, call(): pl.pallas_call(kernel, out_shape=outs, in_specs=[SM] * len(scalars) + [VM...  89.9 us
    all_gather x1, blocking collectives, spread_weights(): columns = lax.all_gather(summed, 'z', axis=0, tiled=False)  66.9 us
    all_to_all x5, starting transfers between devices, plane_exchange(): return lax.all_to_all(a, PLANE, split_axis=0, concat_axis=0, tiled=True)  42.7 us
    all_to_all x1, starting transfers between devices, body(): lax.all_to_all(after(most, code), SPACE, split_axis=0, concat_axis=0, til...  13.1 us
  transfers between devices with their start and end apart: 10, of which 7 were waited for; matrix products, arithmetic and copies ran while one was open for 9% of the time, Pallas kernels for 22%

profile of v2, /device:TPU:2, one launch (start us, length us, event | category | flops | bytes accessed | tf_op | source)
XLA Modules:
  0.0 384.7 jit_solution(18384858505072870427)
XLA Ops:
  7.2 0.7 all-gather.3.cloned.1.call-update
  8.0 0.9 fusion.3
  8.9 0.8 fusion.2
  9.8 0.6 multiply_add_fusion.2
  10.6 0.7 all_to_all.46
  11.3 7.5 %all-to-all-start.6 = ((s32[16,16,1]{1,2,0:T(1,128)}), s32[16,16,1]{1,2,0:T(1,128)S(1)}, u32[]{:S(2)}, u32[]{:S(2)}) async-start(s32[16,16,1]{1,2,0:T(1,128)} %bitcast.8), calls=%async_computation.6 | async-start | bytes 16384 | tf_op jit(solution)/shard_map/all_to_all | solution.py:134
  18.8 1.6 compare_select_fusion.2
  20.4 4.6 %all-to-all-done.6 = s32[16,16,1]{1,2,0:T(1,128)S(1)} async-done(((s32[16,16,1]{1,2,0:T(1,128)}), s32[16,16,1]{1,2,0:T(1,128)S(1)}, u32[]{:S(2)}, u32[]{:S(2)}) %all-to-all-start.6) | async-done | bytes 1056 | tf_op jit(solution)/shard_map/all_to_all | solution.py:134
  25.4 0.7 reduce.6
  26.2 0.7 broadcast_in_dim.40
  26.9 0.7 copy.21
  27.6 13.1 %all-to-all-start.7 = ((s32[128,1,1]{2,1,0:T(1,128)}), s32[128,1,1]{2,1,0:T(1,128)}, u32[]{:S(2)}, u32[]{:S(2)}) async-start(s32[128,1,1]{2,1,0:T(1,128)} %copy.21), calls=%async_computation.7 | async-start | bytes 131072 | tf_op jit(solution)/shard_map/all_to_all | solution.py:182
  40.7 1.5 constant_dynamic-slice_fusion.kern_ref
  42.3 0.7 slice.58.offset
  43.0 0.6 slice.59.block
  43.6 1.5 slice.62.rows_ref
  45.0 6.4 %all-to-all-done.7 = s32[128,1,1]{2,1,0:T(1,128)} async-done(((s32[128,1,1]{2,1,0:T(1,128)}), s32[128,1,1]{2,1,0:T(1,128)}, u32[]{:S(2)}, u32[]{:S(2)}) %all-to-all-start.7) | async-done | bytes 544 | tf_op jit(solution)/shard_map/all_to_all | solution.py:182
  51.5 1.6 reduce_max.29
  53.7 1.3 broadcast_select_fusion.1
  55.2 16.6 %shard_map.112 = bf16[128,128,128]{2,1,0:T(8,128)(2,1)} custom-call(s32[128]{0:T(128)} %slice.58.offset, s32[128]{0:T(128)} %slice.59.block, s32[128,128]{1,0:T(8,128)} %slice.62.rows_ref, bf16[16,128,256]{2,1,0:T(8,128)(2,1)S(1)} %bitcast.39, bf16[27,256,128]{2,1,0:T(8,128)(2,1)S(1)} %copy-done.2), custom_call_target="tpu_custom_call" | custom-call | flops 2147483648 | bytes 7077888 | tf_op jit(solution)/shard_map/pallas_call | solution.py:119
  71.9 206.8 %conditional.1 = (f32[16,128,128]{2,1,0:T(8,128)}, f32[16,128,256]{2,1,0:T(8,128)}, bf16[6912,128]{1,0:T(8,128)(2,1)}, bf16[128,128,128]{2,1,0:T(8,128)(2,1)}) conditional(s32[]{:T(128)} %convert_element_type.46, (s32[192]{0:T(256)S(1)}, s32[192]{0:T(256)S(1)}, s32[192]{0:T(256)S(1)}, s32[192,128]{1,0:T(8,128)S(1)}, s32[256]{0:T(256)S(1)}, ...), branch_computations={%region_4.5_spmd, %region_5.6_spmd} | conditional | flops 4295853056 | bytes 134652032 | solution.py:243
  72.7 5.3 %branch_1_fun.5 = bf16[192,128,128]{2,1,0:T(8,128)(2,1)} custom-call(s32[192]{0:T(256)} %get-tuple-element.216.code, bf16[128,128,128]{2,1,0:T(8,128)(2,1)} %get-tuple-element.79.cot_ref), custom_call_target="tpu_custom_call" | custom-call | bytes 10485760 | tf_op jit(solution)/shard_map/cond/branch_1_fun/pallas_call | solution.py:119
  78.0 6.2 %all-to-all-start.3 = ((bf16[192,128,128]{2,1,0:T(8,128)(2,1)}), bf16[192,128,128]{2,1,0:T(8,128)(2,1)}, u32[]{:S(2)}, u32[]{:S(2)}) async-start(bf16[192,128,128]{2,1,0:T(8,128)(2,1)} %branch_1_fun.5), calls=%async_computation.3 | async-start | bytes 12582912 | tf_op jit(solution)/shard_map/cond/branch_1_fun/all_to_all | solution.py:134
  85.7 0.6 slice.48.rows_ref
  86.3 1.3 copy.23.feat_t_ref
  87.6 0.6 multiply_add_fusion.1.slot
  88.2 5.2 %branch_1_fun.8 = bf16[192,128,128]{2,1,0:T(8,128)(2,1)} custom-call(s32[128]{0:T(128)} %multiply_add_fusion.1.slot, bf16[128,128,128]{2,1,0:T(8,128)(2,1)} %get-tuple-element.93.part_ref), custom_call_target="tpu_custom_call" | custom-call | bytes 10485760 | tf_op jit(solution)/shard_map/cond/branch_1_fun/pallas_call | solution.py:119
  93.5 22.6 %branch_1_fun.6 = (f32[16,128,128]{2,1,0:T(8,128)}, f32[16,128,256]{2,1,0:T(8,128)}, f32[27,256,128]{2,1,0:T(8,128)}) custom-call(s32[64]{0:T(128)} %slice.45.offset, s32[64]{0:T(128)} %slice.46.block, s32[64]{0:T(128)} %slice.47.dest, s32[64,128]{1,0:T(8,128)} %slice.48.rows_ref, bf16[16,128,256]{2,1,0:T(8,128)(2,1)S(1)} %bitcast.45, ...), custom_call_target="tpu_custom_call" | custom-call | flops 2147483648 | bytes 11108352 | tf_op jit(solution)/shard_map/cond/branch_1_fun/pallas_call | solution.py:119
  116.0 44.1 %all-to-all-done.3.up_ref = bf16[192,128,128]{2,1,0:T(8,128)(2,1)} async-done(((bf16[192,128,128]{2,1,0:T(8,128)(2,1)}), bf16[192,128,128]{2,1,0:T(8,128)(2,1)}, u32[]{:S(2)}, u32[]{:S(2)}) %all-to-all-start.3) | async-done | bytes 6291488 | tf_op jit(solution)/shard_map/cond/branch_1_fun/all_to_all | solution.py:134
  160.1 16.3 %all-to-all-start.4 = ((bf16[192,128,128]{2,1,0:T(8,128)(2,1)}), bf16[192,128,128]{2,1,0:T(8,128)(2,1)}, u32[]{:S(2)}, u32[]{:S(2)}) async-start(bf16[192,128,128]{2,1,0:T(8,128)(2,1)} %branch_1_fun.8), calls=%async_computation.4 | async-start | bytes 12582912 | tf_op jit(solution)/shard_map/cond/branch_1_fun/all_to_all | solution.py:134
  176.4 0.6 slice.51.block
  177.5 0.6 slice.52.rows_ref
  178.2 32.9 %branch_1_fun.7 = (f32[16,128,256]{2,1,0:T(8,128)}, f32[27,256,128]{2,1,0:T(8,128)}) custom-call(s32[128]{0:T(128)} %slice.50.offset, s32[128]{0:T(128)} %slice.51.block, s32[128]{0:T(128)} %multiply_add_fusion.1.slot, s32[128,128]{1,0:T(8,128)} %slice.52.rows_ref, bf16[16,256,128]{2,1,0:T(8,128)(2,1)} %copy.23.feat_t_ref, ...), custom_call_target="tpu_custom_call" | custom-call | flops 2147483648 | bytes 20447232 | tf_op jit(solution)/shard_map/cond/branch_1_fun/pallas_call | solution.py:119
  211.1 3.5 convert_element_type.34
  214.6 35.8 %all-to-all-done.4.recv_ref = bf16[192,128,128]{2,1,0:T(8,128)(2,1)} async-done(((bf16[192,128,128]{2,1,0:T(8,128)(2,1)}), bf16[192,128,128]{2,1,0:T(8,128)(2,1)}, u32[]{:S(2)}, u32[]{:S(2)}) %all-to-all-start.4) | async-done | bytes 6291488 | tf_op jit(solution)/shard_map/cond/branch_1_fun/all_to_all | solution.py:134
  250.4 6.6 %all-to-all-start.5 = ((bf16[16,432,128]{2,1,0:T(8,128)(2,1)}), bf16[16,432,128]{2,1,0:T(8,128)(2,1)}, u32[]{:S(2)}, u32[]{:S(2)}) async-start(bf16[16,432,128]{2,1,0:T(8,128)(2,1)} %bitcast.4), calls=%async_computation.5 | async-start | bytes 3538944 | tf_op jit(solution)/shard_map/cond/branch_1_fun/all_to_all | solution.py:134
  257.0 7.3 %branch_1_fun.9 = bf16[128,128,128]{2,1,0:T(8,128)(2,1)} custom-call(s32[192]{0:T(256)} %get-tuple-element.215.code, bf16[192,128,128]{2,1,0:T(8,128)(2,1)} %all-to-all-done.4.recv_ref), custom_call_target="tpu_custom_call" | custom-call | bytes 10485760 | tf_op jit(solution)/shard_map/cond/branch_1_fun/pallas_call | solution.py:119
  264.3 14.4 %all-to-all-done.5 = bf16[16,432,128]{2,1,0:T(8,128)(2,1)} async-done(((bf16[16,432,128]{2,1,0:T(8,128)(2,1)}), bf16[16,432,128]{2,1,0:T(8,128)(2,1)}, u32[]{:S(2)}, u32[]{:S(2)}) %all-to-all-start.5) | async-done | bytes 1769504 | tf_op jit(solution)/shard_map/cond/branch_1_fun/all_to_all | solution.py:134
  278.7 1.7 reduce_sum.34
  280.4 66.9 %all-gather = bf16[3456,128]{1,0:T(8,128)(2,1)S(1)} all-gather(bf16[432,128]{1,0:T(8,128)(2,1)S(1)} %reduce_sum.34), channel_id=2, replica_groups=mesh['x'=4,'y'=4,'z'=8,'chan'=2] {'z'}, dimensions={0}, use_global_device_ids=true | all-gather | bytes 995328 | tf_op jit(solution)/shard_map/all_gather | solution.py:139
  347.5 1.4 broadcast_in_dim.44
  348.9 6.1 %all-to-all-start.8 = ((bf16[16,432,128]{2,1,0:T(8,128)(2,1)}), bf16[16,432,128]{2,1,0:T(8,128)(2,1)}, u32[]{:S(2)}, u32[]{:S(2)}) async-start(bf16[16,432,128]{2,1,0:T(8,128)(2,1)} %broadcast_in_dim.44), calls=%async_computation.9 | async-start | bytes 3538944 | tf_op jit(solution)/shard_map/all_to_all | solution.py:134
  355.0 1.3 dynamic-slice_convert_fusion
  356.4 1.9 collective-permute-done.1
  358.3 2.3 add_convert_fusion
  360.6 11.4 %all-to-all-done.8 = bf16[16,432,128]{2,1,0:T(8,128)(2,1)} async-done(((bf16[16,432,128]{2,1,0:T(8,128)(2,1)}), bf16[16,432,128]{2,1,0:T(8,128)(2,1)}, u32[]{:S(2)}, u32[]{:S(2)}) %all-to-all-start.8) | async-done | bytes 1769504 | tf_op jit(solution)/shard_map/all_to_all | solution.py:134
  372.1 3.5 convert_multiply_fusion
  375.6 2.3 add_convert_fusion.1
  (45 shorter events, 4.2 us)
Async XLA Ops:
  7.2 33.6 %copy-start = (bf16[27,256,256]{2,1,0:T(8,128)(2,1)S(1)}, bf16[27,256,256]{2,1,0:T(8,128)(2,1)}, u32[]{:S(2)}) copy-start(bf16[27,256,256]{2,1,0:T(8,128)(2,1)} %param.12) | copy-start | bytes 10616836
  7.2 64.7 %all-gather.3.cloned.1.call-start = ((), (), s32[]{:S(2)}) async-start(), calls=%async_computation.10 | async-start | bytes 4718592 | tf_op jit(solution)/shard_map/all_gather | solution.py:168
  7.9 45.8 %collective-permute-start = (bf16[2048,128]{1,0:T(8,128)(2,1)}, bf16[2048,128]{1,0:T(8,128)(2,1)}, u32[]{:S(2)}, u32[]{:S(2)}) collective-permute-start(bf16[2048,128]{1,0:T(8,128)(2,1)} %param.11), channel_id=1, source_target_pairs={{0,1},{1,0},{2,3},{3,2},{4,5},{5,4},{6,7},{7,6},{8,9},{9,8},{10,11... | collective-permute-start | bytes 1572872 | tf_op jit(solution)/shard_map/ppermute | solution.py:187
  9.7 0.8 copy-start.5
  9.8 0.6 copy-start.7
  11.3 13.6 %all-to-all-start.6 = ((s32[16,16,1]{1,2,0:T(1,128)}), s32[16,16,1]{1,2,0:T(1,128)S(1)}, u32[]{:S(2)}, u32[]{:S(2)}) async-start(s32[16,16,1]{1,2,0:T(1,128)} %bitcast.8), calls=%async_computation.6 | async-start | bytes 16384 | tf_op jit(solution)/shard_map/all_to_all | solution.py:134
  26.2 16.1 %copy-start.10 = (s32[192]{0:T(256)S(1)}, s32[192]{0:T(256)}, u32[]{:S(2)}) copy-start(s32[192]{0:T(256)} %param.14) | copy-start | bytes 2308
  26.2 16.8 %copy-start.11 = (s32[192]{0:T(256)S(1)}, s32[192]{0:T(256)}, u32[]{:S(2)}) copy-start(s32[192]{0:T(256)} %param.15) | copy-start | bytes 2308
  27.6 23.9 %all-to-all-start.7 = ((s32[128,1,1]{2,1,0:T(1,128)}), s32[128,1,1]{2,1,0:T(1,128)}, u32[]{:S(2)}, u32[]{:S(2)}) async-start(s32[128,1,1]{2,1,0:T(1,128)} %copy.21), calls=%async_computation.7 | async-start | bytes 131072 | tf_op jit(solution)/shard_map/all_to_all | solution.py:182
  40.7 334.9 %reduce-scatter.2.cloned.1.call-start = ((), (), s32[]{:S(2)}) async-start(), calls=%async_computation.11 | async-start | bytes 4718592 | tf_op jit(solution)/shard_map/reduce_scatter | solution.py:247
  42.3 12.9 %copy-start.2 = (bf16[27,256,128]{2,1,0:T(8,128)(2,1)S(1)}, bf16[27,256,128]{2,1,0:T(8,128)(2,1)}, u32[]{:S(2)}) copy-start(bf16[27,256,128]{2,1,0:T(8,128)(2,1)} %constant_dynamic-slice_fusion.kern_ref) | copy-start | bytes 5308420
  55.2 16.7 %copy-start.3 = (s32[192,128]{1,0:T(8,128)S(1)}, s32[192,128]{1,0:T(8,128)}, u32[]{:S(2)}) copy-start(s32[192,128]{1,0:T(8,128)} %compare_select_fusion.2) | copy-start | bytes 294916
  55.2 16.7 %copy-start.4 = (bf16[2048,128]{1,0:T(8,128)(2,1)S(1)}, bf16[2048,128]{1,0:T(8,128)(2,1)}, u32[]{:S(2)}) copy-start(bf16[2048,128]{1,0:T(8,128)(2,1)} %param.13) | copy-start | bytes 1572868
  55.2 16.7 %copy-start.6 = (s32[128]{0:T(128)S(1)}, s32[128]{0:T(128)}, u32[]{:S(2)}) copy-start(s32[128]{0:T(128)} %copy-done.5) | copy-start | bytes 1540
  55.2 16.7 %copy-start.8 = (s32[128]{0:T(128)S(1)}, s32[128]{0:T(128)}, u32[]{:S(2)}) copy-start(s32[128]{0:T(128)} %copy-done.7) | copy-start | bytes 1540
  55.2 16.7 %copy-start.9 = (s32[192]{0:T(256)S(1)}, s32[192]{0:T(256)}, u32[]{:S(2)}) copy-start(s32[192]{0:T(256)} %param.18) | copy-start | bytes 2308
  78.0 82.1 %all-to-all-start.3 = ((bf16[192,128,128]{2,1,0:T(8,128)(2,1)}), bf16[192,128,128]{2,1,0:T(8,128)(2,1)}, u32[]{:S(2)}, u32[]{:S(2)}) async-start(bf16[192,128,128]{2,1,0:T(8,128)(2,1)} %branch_1_fun.5), calls=%async_computation.3 | async-start | bytes 12582912 | tf_op jit(solution)/shard_map/cond/branch_1_fun/all_to_all | solution.py:134
  160.1 90.3 %all-to-all-start.4 = ((bf16[192,128,128]{2,1,0:T(8,128)(2,1)}), bf16[192,128,128]{2,1,0:T(8,128)(2,1)}, u32[]{:S(2)}, u32[]{:S(2)}) async-start(bf16[192,128,128]{2,1,0:T(8,128)(2,1)} %branch_1_fun.8), calls=%async_computation.4 | async-start | bytes 12582912 | tf_op jit(solution)/shard_map/cond/branch_1_fun/all_to_all | solution.py:134
  250.4 28.2 %all-to-all-start.5 = ((bf16[16,432,128]{2,1,0:T(8,128)(2,1)}), bf16[16,432,128]{2,1,0:T(8,128)(2,1)}, u32[]{:S(2)}, u32[]{:S(2)}) async-start(bf16[16,432,128]{2,1,0:T(8,128)(2,1)} %bitcast.4), calls=%async_computation.5 | async-start | bytes 3538944 | tf_op jit(solution)/shard_map/cond/branch_1_fun/all_to_all | solution.py:134
  348.9 23.1 %all-to-all-start.8 = ((bf16[16,432,128]{2,1,0:T(8,128)(2,1)}), bf16[16,432,128]{2,1,0:T(8,128)(2,1)}, u32[]{:S(2)}, u32[]{:S(2)}) async-start(bf16[16,432,128]{2,1,0:T(8,128)(2,1)} %broadcast_in_dim.44), calls=%async_computation.9 | async-start | bytes 3538944 | tf_op jit(solution)/shard_map/all_to_all | solution.py:134
  356.3 2.0 collective-permute-start.1
  358.3 19.5 %copy-start.1 = (bf16[27,256,256]{2,1,0:T(8,128)(2,1)S(1)}, bf16[27,256,256]{2,1,0:T(8,128)(2,1)}, u32[]{:S(2)}) copy-start(bf16[27,256,256]{2,1,0:T(8,128)(2,1)} %param.12) | copy-start | bytes 10616836
Sparse Core Ops, SparseCore 0:
  9.8 59.1 all-gather.2
  278.8 95.8 reduce-scatter.1
